TPU v7x, 256 devices: a whole 4x4x8 slice. The times are simulated.
256 devices in a mesh: wide: 32 (over y, x, core), narrow: 8 (over z).
Axes of the slice: x: 4, y: 4, z: 8, core: 2. Of those that a mesh axis runs over, the one named last changes fastest.
Arguments:
- constraint_rows: bfloat16 [512, 256, 1024], P(None, ('wide', 'narrow')), may hold values from -1 to 1
- metric: bfloat16 [1024, 1024], replicated, may hold values from -8 to 8, as said below
Outputs:
- factored: float32 [512, 256, 8, 128], P(None, 'wide', 'narrow')
Inputs may be any that keep to these rules, and one draw needn't show every extreme that they name: `metric`: symmetric and positive definite.
All inputs are finite; a program needn't handle non-finite values.
Results may differ from a plain program's by a relative error of at most 0.0052.
Values may be sent and summed in bfloat16 or wider, within the bound.
No kernel may reach another device: no remote copies, remote signals or barrier semaphores. Data moves between devices by JAX's collectives and lax.ppermute only.
A program may use at most 64 MiB of HBM per device.

v0:
```python
import jax
import jax.numpy as jnp
from jax import lax
from jax.sharding import PartitionSpec as P

P_SIZE = 1024
PB = 256
NPANEL = 2


def left_solve(factor_low, right_side):
    return jax.scipy.linalg.solve_triangular(factor_low, right_side, lower=True)


def strip_major(schur_slab, strips):
    row_count = schur_slab.shape[0]
    strip_len = schur_slab.shape[1] // strips
    reordered = schur_slab.reshape(row_count, strip_len, strips).transpose(0, 2, 1)
    return reordered.reshape(row_count, 1, strips, strip_len)


def local(constraint_rows, metric):
    groups = lax.axis_size(("wide", "narrow"))
    strips = lax.axis_size("narrow")
    row_count = constraint_rows.shape[0]
    panel_depth = P_SIZE // groups
    block_rows = PB // groups
    flat_rows = constraint_rows[:, 0, :]
    projected = jnp.dot(flat_rows, metric, preferred_element_type=jnp.float32).astype(jnp.bfloat16)
    gram_cols = jnp.einsum(
        "rn,kmn->rkm",
        projected,
        lax.all_gather(constraint_rows[:panel_depth], ("wide", "narrow"), axis=1, tiled=True),
        preferred_element_type=jnp.float32,
    )
    schur_slab = (gram_cols * gram_cols).reshape(row_count, P_SIZE)
    grid_block = lax.all_to_all(
        strip_major(schur_slab, strips), "narrow", split_axis=2, concat_axis=1, tiled=True
    )
    strip_len = P_SIZE // strips
    grid_rows = row_count * strips
    narrow_panel = PB // strips
    own_strip = lax.axis_index("narrow")
    flat_block = grid_block.reshape(grid_rows, strip_len)
    for panel_number in range(NPANEL):
        col_begin = panel_number * PB
        row_begin = col_begin // groups
        strip_begin = col_begin // strips
        strip_end = strip_begin + narrow_panel
        own_rows = flat_block.reshape(row_count, strips, strip_len)[
            row_begin : row_begin + block_rows, :, strip_begin:
        ]
        shared = lax.all_gather(own_rows, "wide", axis=1, tiled=True)
        shared = shared.reshape(PB, strip_len - strip_begin)
        diag_strip, row_strip = (
            lax.all_gather(shared[:, :narrow_panel], "narrow", axis=1, tiled=True),
            lax.all_gather(flat_block[:, strip_begin:strip_end], "narrow", axis=1, tiled=True),
        )
        diag_block = diag_strip.reshape(PB, strips, narrow_panel).transpose(0, 2, 1).reshape(PB, PB)
        panel_cols = (
            row_strip.reshape(grid_rows, strips, narrow_panel)
            .transpose(0, 2, 1)
            .reshape(grid_rows, PB)
        )
        factor_low = jnp.linalg.cholesky(diag_block)
        upper_part = left_solve(factor_low, shared[:, narrow_panel:])
        column = left_solve(factor_low, panel_cols.T).T
        trailing = flat_block[:, strip_end:] - jnp.dot(
            column, upper_part, precision=lax.Precision.HIGHEST
        )
        own_cols = lax.dynamic_index_in_dim(
            column.reshape(grid_rows, narrow_panel, strips), own_strip, 2, keepdims=False
        )
        flat_block = jnp.concatenate([flat_block[:, :strip_begin], own_cols, trailing], axis=1)
    return flat_block.reshape(row_count, strips, 1, strip_len)


def solution(mesh):
    placed = (P(None, ("wide", "narrow"), None), P())
    return jax.shard_map(
        local,
        mesh=mesh,
        in_specs=placed,
        out_specs=P(None, "wide", "narrow", None),
        check_vma=False,
    )
```

profile of v0, /device:TPU:4, one launch (start us, length us, event | category | flops | bytes accessed | tf_op | source)
XLA Modules:
  0.0 463.7 jit_solution(18273028846116087548)
XLA Ops:
  8.1 110.0 %all-gather.6.cloned.1.call-done = bf16[4,256,1024]{2,0,1:T(4,128)(2,1)} async-done(((bf16[4,1,1024]{2,0,1:T(4,128)(2,1)}), bf16[4,256,1024]{2,0,1:T(4,128)(2,1)}) %all-gather.6.cloned.1.call-update) | async-done | bytes 2097168 | tf_op jit(solution)/shard_map/all_gather | solution.py:33
  118.1 5.7 %fusion.8 = f32[512,4,256]{0,2,1:T(8,128)} fusion(bf16[4,256,1024]{2,0,1:T(4,128)(2,1)} %all-gather.6.cloned.1.call-done, bf16[1024,1024]{1,0:T(8,128)(2,1)S(1)} %copy-done, bf16[512,1,1024]{2,0,1:T(8,128)(2,1)} %param.5), kind=kOutput, calls=%fused_computation.22 | convolution fusion | flops 2148532224 | bytes 7340032 | tf_op jit(solution)/shard_map/rn,kmn->rkm/dot_general | solution.py:30
  123.8 2.0 copy.62
  125.8 56.3 %all_to_all.4 = f32[512,1,8,128]{3,1,0,2:T(1,128)S(1)} all-to-all(f32[512,1,8,128]{3,1,0,2:T(1,128)S(1)} %bitcast.153), channel_id=1, replica_groups=mesh['wide'=32,'narrow'=8] {'narrow'}, dimensions={2} | all-to-all | bytes 4194304 | tf_op jit(solution)/shard_map/all_to_all | solution.py:37
  184.9 1.9 slice.153
  186.8 23.0 %all-gather = f32[1,1,256,128]{3,2,1,0:T(8,128)S(1)} all-gather(f32[1,1,8,128]{3,2,1,0:T(8,128)S(1)} %bitcast.150), channel_id=2, replica_groups=mesh['wide'=32,'narrow'=8] {'wide'}, dimensions={2}, use_global_device_ids=true | all-gather | bytes 135168 | tf_op jit(solution)/shard_map/all_gather | solution.py:53
  210.1 26.7 %all_gather.23 = f32[256,256]{0,1:T(8,128)S(1)} all-gather(f32[256,32]{0,1:T(8,128)S(1)} %copy.64), channel_id=1, replica_groups=mesh['wide'=32,'narrow'=8] {'narrow'}, dimensions={1}, use_global_device_ids=true | all-gather | bytes 294912 | tf_op jit(solution)/shard_map/all_gather | solution.py:56
  237.3 11.7 %cholesky.130 = f32[128,128]{1,0:T(8,128)S(1)} custom-call(f32[128,128]{1,0:T(8,128)S(1)} %cholesky.194), custom_call_target="Cholesky" | custom-call | tf_op jit(solution)/shard_map/jit(cholesky)/cholesky | solution.py:65
  249.1 9.8 %custom-call.23 = f32[1,128,128]{1,2,0:T(8,128)S(1)} custom-call(f32[1,128,128]{2,1,0:T(8,128)S(1)} %get-tuple-element.66), custom_call_target="InvertDiagBlocksLowerTriangular" | custom-call | tf_op jit(solution)/shard_map/jit(cholesky)/cholesky | solution.py:65
  259.4 11.7 %cholesky.147 = f32[128,128]{1,0:T(8,128)S(1)} custom-call(f32[128,128]{1,0:T(8,128)S(1)} %convolution_subtract_fusion.5), custom_call_target="Cholesky" | custom-call | tf_op jit(solution)/shard_map/jit(cholesky)/cholesky | solution.py:65
  273.2 3.9 while.6
  277.1 19.7 %custom-call.24 = f32[2,128,128]{1,2,0:T(8,128)S(1)} custom-call(f32[2,128,128]{2,1,0:T(8,128)S(1)} %get-tuple-element.37), custom_call_target="InvertDiagBlocksLowerTriangular" | custom-call | tf_op jit(solution)/shard_map/jit(_solve_triangular)/triangular_solve | solution.py:12
  296.8 2.1 copy.83
  299.8 4.6 copy.99
  306.3 2.0 convolution_subtract_fusion.1
  308.3 1.9 fusion.34
  310.3 2.7 convolution_subtract_fusion.2
  316.0 24.0 %all-gather.1 = f32[256,96]{1,0:T(8,128)S(1)} all-gather(f32[8,96]{1,0:T(8,128)S(1)} %copy.73), channel_id=3, replica_groups=mesh['wide'=32,'narrow'=8] {'wide'}, dimensions={0}, use_global_device_ids=true | all-gather | bytes 101376 | tf_op jit(solution)/shard_map/all_gather | solution.py:53
  340.2 26.5 %all_gather.26 = f32[256,256]{0,1:T(8,128)S(1)} all-gather(f32[256,32]{0,1:T(8,128)S(1)} %copy.85), channel_id=1, replica_groups=mesh['wide'=32,'narrow'=8] {'narrow'}, dimensions={1}, use_global_device_ids=true | all-gather | bytes 294912 | tf_op jit(solution)/shard_map/all_gather | solution.py:56
  367.2 11.7 %cholesky.164 = f32[128,128]{1,0:T(8,128)S(1)} custom-call(f32[128,128]{1,0:T(8,128)S(1)} %cholesky.197), custom_call_target="Cholesky" | custom-call | tf_op jit(solution)/shard_map/jit(cholesky)/cholesky | solution.py:65
  378.9 9.8 %custom-call.25 = f32[1,128,128]{1,2,0:T(8,128)S(1)} custom-call(f32[1,128,128]{2,1,0:T(8,128)S(1)} %get-tuple-element.62), custom_call_target="InvertDiagBlocksLowerTriangular" | custom-call | tf_op jit(solution)/shard_map/jit(cholesky)/cholesky | solution.py:65
  389.3 11.7 %cholesky.181 = f32[128,128]{1,0:T(8,128)S(1)} custom-call(f32[128,128]{1,0:T(8,128)S(1)} %convolution_subtract_fusion.4), custom_call_target="Cholesky" | custom-call | tf_op jit(solution)/shard_map/jit(cholesky)/cholesky | solution.py:65
  403.6 3.9 while.7
  407.5 19.7 %custom-call.26 = f32[2,128,128]{1,2,0:T(8,128)S(1)} custom-call(f32[2,128,128]{2,1,0:T(8,128)S(1)} %get-tuple-element.38), custom_call_target="InvertDiagBlocksLowerTriangular" | custom-call | tf_op jit(solution)/shard_map/jit(_solve_triangular)/triangular_solve | solution.py:12
  427.2 2.0 fusion.1
  429.7 1.9 copy.70
  432.5 4.6 copy.98
  439.0 2.0 convolution_subtract_fusion
  441.0 1.9 fusion.36
  444.4 2.9 convolution_subtract_fusion.3
  447.7 2.0 copy.80
  451.5 5.5 %pad_maximum_fusion.4 = f32[512,8,1,128]{3,1,0,2:T(8,128)} fusion(f32[512,8,1,64]{3,1,0,2:T(8,128)} %bitcast.154, f32[512,8,1,32]{3,1,0,2:T(8,128)} %bitcast.152, f32[512,8,1,32]{3,1,0,2:T(8,128)} %bitcast.151), kind=kLoop, calls=%fused_computation.18 | loop fusion | flops 1048576 | bytes 4194304 | tf_op jit(solution)/shard_map/concatenate | solution.py:74
  (89 shorter events, 29.2 us)
Async XLA Ops:
  6.5 111.6 %copy-start = (bf16[1024,1024]{1,0:T(8,128)(2,1)S(1)}, bf16[1024,1024]{1,0:T(8,128)(2,1)}, u32[]{:S(2)}) copy-start(bf16[1024,1024]{1,0:T(8,128)(2,1)} %param.6) | copy-start | bytes 6291460
  6.5 111.6 %all-gather.6.cloned.1.call-start = ((), (), s32[]{:S(2)}) async-start(), calls=%async_computation.1 | async-start | bytes 2105344 | tf_op jit(solution)/shard_map/all_gather | solution.py:33
  8.0 291.7 %all-gather.8.cloned.1.call-start = ((), (), s32[]{:S(2)}) async-start(), calls=%async_computation.2 | async-start | bytes 4718592 | tf_op jit(solution)/shard_map/all_gather | solution.py:57
  182.1 1.3 copy-start.3
  184.8 247.6 %all-gather.10.cloned.1.call-start = ((), (), s32[]{:S(2)}) async-start(), calls=%async_computation.3 | async-start | bytes 4718592 | tf_op jit(solution)/shard_map/all_gather | solution.py:57
  184.9 1.9 slice-start
  237.0 59.8 %copy-start.4 = (f32[4096,96]{1,0:T(8,128)S(1)}, f32[4096,96]{1,0:T(8,128)}, u32[]{:S(2)}) copy-start(f32[4096,96]{1,0:T(8,128)} %slice.153) | copy-start | bytes 4718596
  308.3 2.0 copy-start.7
  310.3 2.8 copy-start.2
  313.0 1.1 copy-start.5
  442.9 1.4 copy-start.6
  451.5 5.5 %copy-start.1 = (bf16[1024,1024]{1,0:T(8,128)(2,1)S(1)}, bf16[1024,1024]{1,0:T(8,128)(2,1)}, u32[]{:S(2)}) copy-start(bf16[1024,1024]{1,0:T(8,128)(2,1)} %param.6) | copy-start | bytes 6291460
Sparse Core Ops, SparseCore 0:
  11.1 107.0 all-gather.5
  184.9 53.2 all-gather.7
  315.2 53.6 all-gather.9
where the time goes:
time: 469 us; the launch traced here: 464 us
  blocking collectives  157 us (33%)
  other arithmetic  116 us (25%)
  waiting for transfers between devices  110 us (23%)
  local copies, waits for them, and re-layouts  38.8 us (8%)
  matrix products  25.5 us (5%)
  between operations  16.2 us (3%)
    all_gather x1, waiting for transfers between devices, local(): lax.all_gather(constraint_rows[:panel_depth], ('wide', 'narrow'), axis=1,...  110 us
    another operation x13, other arithmetic, local(): factor_low = jnp.linalg.cholesky(diag_block)  68.6 us
    all_to_all x1, blocking collectives, local(): lax.all_to_all(strip_major(schur_slab, strips), 'narrow', split_axis=2, c...  56.3 us
    all_gather x2, blocking collectives, local(): lax.all_gather(shared[:, :narrow_panel], 'narrow', axis=1, tiled=True)  53.2 us
    all_gather x2, blocking collectives, local(): shared = lax.all_gather(own_rows, 'wide', axis=1, tiled=True)  47 us
    another operation x5, other arithmetic, left_solve(): return jax.scipy.linalg.solve_triangular(factor_low, right_side, lower=True)  39.4 us
    another operation x12, matrix products, left_solve(): return jax.scipy.linalg.solve_triangular(factor_low, right_side, lower=True)  13.2 us
  transfers between devices with their start and end apart: 3, of which 1 were waited for; matrix products, arithmetic and copies ran while one was open for 28% of the time, Pallas kernels for 0%

commit v1 on v0

--- a/solution.py
+++ b/solution.py
@@ -30,7 +30,15 @@
     gram_cols = jnp.einsum(
         "rn,kmn->rkm",
         projected,
-        lax.all_gather(constraint_rows[:panel_depth], ("wide", "narrow"), axis=1, tiled=True),
+        jnp.concatenate(
+            lax.all_to_all(
+                jnp.stack([constraint_rows[:panel_depth]] * lax.axis_size(("wide", "narrow"))),
+                ("wide", "narrow"),
+                0,
+                0,
+            ),
+            axis=1,
+        ),
         preferred_element_type=jnp.float32,
     )
     schur_slab = (gram_cols * gram_cols).reshape(row_count, P_SIZE)

time: 469 us -> 425 us (0.906)
  waiting for transfers between devices: 110 us -> 0.07 us
  blocking collectives: 157 us -> 221 us
    all_gather x1 -> x0, waiting for transfers between devices: 110 us -> none  [local(): lax.all_gather(constraint_rows[:panel_depth], ('wide', 'narrow'), axis=1,...]
    all_to_all x0 -> x1, blocking collectives: none -> 66.8 us  [local(): lax.all_to_all(jnp.stack([constraint_rows[:panel_depth]] * lax.axis_size(...]
  transfers between devices with their start and end apart: 3 -> 2, of which waited for: 1 -> 0; matrix products, arithmetic and copies ran while one was open for 28% -> 31% of each run, Pallas kernels for 0% -> 0%
where the time goes in v1:
time: 425 us; the launch traced here: 419 us
  blocking collectives  221 us (52%)
  other arithmetic  116 us (27%)
  local copies, waits for them, and re-layouts  39.3 us (9%)
  matrix products  25.2 us (6%)
  between operations  16.8 us (4%)
    another operation x13, other arithmetic, local(): factor_low = jnp.linalg.cholesky(diag_block)  68.7 us
    all_to_all x1, blocking collectives, local(): lax.all_to_all(jnp.stack([constraint_rows[:panel_depth]] * lax.axis_size(...  66.8 us
    all_to_all x1, blocking collectives, local(): lax.all_to_all(strip_major(schur_slab, strips), 'narrow', split_axis=2, c...  55.1 us
    all_gather x2, blocking collectives, local(): lax.all_gather(shared[:, :narrow_panel], 'narrow', axis=1, tiled=True)  53 us
    all_gather x2, blocking collectives, local(): shared = lax.all_gather(own_rows, 'wide', axis=1, tiled=True)  45.8 us
    another operation x5, other arithmetic, left_solve(): return jax.scipy.linalg.solve_triangular(factor_low, right_side, lower=True)  39.4 us
    another operation x12, matrix products, left_solve(): return jax.scipy.linalg.solve_triangular(factor_low, right_side, lower=True)  13.2 us
  transfers between devices with their start and end apart: 2, of which 0 were waited for; matrix products, arithmetic and copies ran while one was open for 31% of the time, Pallas kernels for 0%

profile of v1, /device:TPU:4, one launch (start us, length us, event | category | flops | bytes accessed | tf_op | source)
XLA Modules:
  0.0 418.6 jit_solution(18414694765294300255)
XLA Ops:
  8.0 66.8 %all_to_all.14 = bf16[256,4,1,1024]{3,1,2,0:T(4,128)(2,1)} all-to-all(bf16[256,4,1,1024]{3,1,2,0:T(4,128)(2,1)S(1)} %stack.2), channel_id=1, replica_groups=mesh['wide'=32,'narrow'=8] {'wide','narrow'}, dimensions={0} | all-to-all | bytes 4194304 | tf_op jit(solution)/shard_map/all_to_all | solution.py:34
  74.8 5.4 %fusion.9 = f32[512,4,256]{0,2,1:T(8,128)} fusion(bf16[256,4,1,1024]{3,1,2,0:T(4,128)(2,1)} %all_to_all.14, bf16[1024,1024]{1,0:T(8,128)(2,1)S(1)} %copy-done, bf16[512,1,1024]{2,0,1:T(8,128)(2,1)S(1)} %copy-done.8), kind=kOutput, calls=%fused_computation.23 | convolution fusion | flops 2148532224 | bytes 7340032 | tf_op jit(solution)/shard_map/rn,kmn->rkm/dot_general | solution.py:30
  80.1 2.0 copy.59
  82.1 55.1 %all_to_all.15 = f32[512,1,8,128]{3,1,0,2:T(1,128)S(1)} all-to-all(f32[512,1,8,128]{3,1,0,2:T(1,128)S(1)} %bitcast.162), channel_id=1, replica_groups=mesh['wide'=32,'narrow'=8] {'narrow'}, dimensions={2} | all-to-all | bytes 4194304 | tf_op jit(solution)/shard_map/all_to_all | solution.py:45
  140.0 1.9 slice.156
  141.9 21.9 %all-gather = f32[1,1,256,128]{3,2,1,0:T(8,128)S(1)} all-gather(f32[1,1,8,128]{3,2,1,0:T(8,128)S(1)} %bitcast.159), channel_id=2, replica_groups=mesh['wide'=32,'narrow'=8] {'wide'}, dimensions={2}, use_global_device_ids=true | all-gather | bytes 135168 | tf_op jit(solution)/shard_map/all_gather | solution.py:61
  164.1 26.5 %all_gather.19 = f32[256,256]{0,1:T(8,128)S(1)} all-gather(f32[256,32]{0,1:T(8,128)S(1)} %copy.61), channel_id=1, replica_groups=mesh['wide'=32,'narrow'=8] {'narrow'}, dimensions={1}, use_global_device_ids=true | all-gather | bytes 294912 | tf_op jit(solution)/shard_map/all_gather | solution.py:64
  191.1 11.7 %cholesky.130 = f32[128,128]{1,0:T(8,128)S(1)} custom-call(f32[128,128]{1,0:T(8,128)S(1)} %cholesky.194), custom_call_target="Cholesky" | custom-call | tf_op jit(solution)/shard_map/jit(cholesky)/cholesky | solution.py:73
  202.9 9.8 %custom-call.23 = f32[1,128,128]{1,2,0:T(8,128)S(1)} custom-call(f32[1,128,128]{2,1,0:T(8,128)S(1)} %get-tuple-element.66), custom_call_target="InvertDiagBlocksLowerTriangular" | custom-call | tf_op jit(solution)/shard_map/jit(cholesky)/cholesky | solution.py:73
  213.2 11.7 %cholesky.147 = f32[128,128]{1,0:T(8,128)S(1)} custom-call(f32[128,128]{1,0:T(8,128)S(1)} %convolution_subtract_fusion.5), custom_call_target="Cholesky" | custom-call | tf_op jit(solution)/shard_map/jit(cholesky)/cholesky | solution.py:73
  227.1 4.2 while.6
  231.3 19.7 %custom-call.24 = f32[2,128,128]{1,2,0:T(8,128)S(1)} custom-call(f32[2,128,128]{2,1,0:T(8,128)S(1)} %get-tuple-element.37), custom_call_target="InvertDiagBlocksLowerTriangular" | custom-call | tf_op jit(solution)/shard_map/jit(_solve_triangular)/triangular_solve | solution.py:12
  251.0 2.1 copy.80
  254.0 4.6 %copy.98 = f32[4096,32,8]{0,2,1:T(8,128)S(1)} copy(f32[4096,32,8]{0,1,2:T(8,128)} %bitcast.165) | data formatting | bytes 8388608 | tf_op jit(solution)/shard_map/transpose | solution.py:70
  260.5 2.0 convolution_subtract_fusion.1
  262.5 1.9 fusion.35
  264.5 2.7 convolution_subtract_fusion.2
  270.2 23.9 %all-gather.1 = f32[256,96]{1,0:T(8,128)S(1)} all-gather(f32[8,96]{1,0:T(8,128)S(1)} %copy.70), channel_id=3, replica_groups=mesh['wide'=32,'narrow'=8] {'wide'}, dimensions={0}, use_global_device_ids=true | all-gather | bytes 101376 | tf_op jit(solution)/shard_map/all_gather | solution.py:61
  294.3 26.5 %all_gather.22 = f32[256,256]{0,1:T(8,128)S(1)} all-gather(f32[256,32]{0,1:T(8,128)S(1)} %copy.82), channel_id=1, replica_groups=mesh['wide'=32,'narrow'=8] {'narrow'}, dimensions={1}, use_global_device_ids=true | all-gather | bytes 294912 | tf_op jit(solution)/shard_map/all_gather | solution.py:64
  321.3 11.7 %cholesky.164 = f32[128,128]{1,0:T(8,128)S(1)} custom-call(f32[128,128]{1,0:T(8,128)S(1)} %cholesky.197), custom_call_target="Cholesky" | custom-call | tf_op jit(solution)/shard_map/jit(cholesky)/cholesky | solution.py:73
  333.1 9.8 %custom-call.25 = f32[1,128,128]{1,2,0:T(8,128)S(1)} custom-call(f32[1,128,128]{2,1,0:T(8,128)S(1)} %get-tuple-element.62), custom_call_target="InvertDiagBlocksLowerTriangular" | custom-call | tf_op jit(solution)/shard_map/jit(cholesky)/cholesky | solution.py:73
  343.4 11.7 %cholesky.181 = f32[128,128]{1,0:T(8,128)S(1)} custom-call(f32[128,128]{1,0:T(8,128)S(1)} %convolution_subtract_fusion.4), custom_call_target="Cholesky" | custom-call | tf_op jit(solution)/shard_map/jit(cholesky)/cholesky | solution.py:73
  357.9 4.1 while.7
  362.0 19.7 %custom-call.26 = f32[2,128,128]{1,2,0:T(8,128)S(1)} custom-call(f32[2,128,128]{2,1,0:T(8,128)S(1)} %get-tuple-element.38), custom_call_target="InvertDiagBlocksLowerTriangular" | custom-call | tf_op jit(solution)/shard_map/jit(_solve_triangular)/triangular_solve | solution.py:12
  381.7 2.0 fusion.1
  384.2 2.0 copy.67
  387.0 4.6 %copy.97 = f32[4096,8,32]{0,1,2:T(8,128)S(1)} copy(f32[4096,8,32]{0,2,1:T(8,128)} %bitcast.164) | data formatting | bytes 8388608 | tf_op jit(solution)/shard_map/reshape | solution.py:69
  393.5 2.0 convolution_subtract_fusion
  395.5 1.9 fusion.37
  398.9 2.9 convolution_subtract_fusion.3
  402.3 1.9 copy.77
  405.9 5.5 %pad_maximum_fusion.4 = f32[512,8,1,128]{3,1,0,2:T(8,128)} fusion(f32[512,8,1,64]{3,1,0,2:T(8,128)} %bitcast.163, f32[512,8,1,32]{3,1,0,2:T(8,128)} %bitcast.161, f32[512,8,1,32]{3,1,0,2:T(8,128)} %bitcast.160), kind=kLoop, calls=%fused_computation.18 | loop fusion | flops 1048576 | bytes 4194304 | tf_op jit(solution)/shard_map/concatenate | solution.py:82
  (90 shorter events, 29.7 us)
Async XLA Ops:
  6.5 68.2 %copy-start = (bf16[1024,1024]{1,0:T(8,128)(2,1)S(1)}, bf16[1024,1024]{1,0:T(8,128)(2,1)}, u32[]{:S(2)}) copy-start(bf16[1024,1024]{1,0:T(8,128)(2,1)} %param.6) | copy-start | bytes 6291460
  6.5 247.4 %all-gather.5.cloned.1.call-start = ((), (), s32[]{:S(2)}) async-start(), calls=%async_computation.2 | async-start | bytes 4718592 | tf_op jit(solution)/shard_map/all_gather | solution.py:65
  8.0 66.8 %copy-start.8 = (bf16[512,1,1024]{2,0,1:T(8,128)(2,1)S(1)}, bf16[512,1,1024]{2,0,1:T(8,128)(2,1)}, u32[]{:S(2)}) copy-start(bf16[512,1,1024]{2,0,1:T(8,128)(2,1)} %param.5) | copy-start | bytes 3145732
  137.2 1.3 copy-start.3
  139.9 247.0 %all-gather.7.cloned.1.call-start = ((), (), s32[]{:S(2)}) async-start(), calls=%async_computation.3 | async-start | bytes 4718592 | tf_op jit(solution)/shard_map/all_gather | solution.py:65
  140.0 1.9 slice-start
  190.8 60.2 %copy-start.4 = (f32[4096,96]{1,0:T(8,128)S(1)}, f32[4096,96]{1,0:T(8,128)}, u32[]{:S(2)}) copy-start(f32[4096,96]{1,0:T(8,128)} %slice.156) | copy-start | bytes 4718596
  262.5 2.0 copy-start.7
  264.5 2.8 copy-start.2
  267.2 1.1 copy-start.5
  397.5 1.4 copy-start.6
  405.9 5.5 %copy-start.1 = (bf16[1024,1024]{1,0:T(8,128)(2,1)S(1)}, bf16[1024,1024]{1,0:T(8,128)(2,1)}, u32[]{:S(2)}) copy-start(bf16[1024,1024]{1,0:T(8,128)(2,1)} %param.6) | copy-start | bytes 6291460
Sparse Core Ops, SparseCore 0:
  140.1 51.4 all-gather.4
  269.4 53.5 all-gather.6
